TPU v7x, 32 devices: a whole 2x2x4 slice. The times are simulated.
32 devices in a mesh: dp: 2 (over x), expert: 16 (over z, y, core).
Axes of the slice: x: 2, y: 2, z: 4, core: 2. Of those that a mesh axis runs over, the one named last changes fastest.
Arguments:
- tokens: bfloat16 [4096, 1024], P(('dp', 'expert')), may hold values from -6 to 6
- cotangent: bfloat16 [4096, 1024], P(('dp', 'expert')), may hold values from -6 to 6
- expert_ids: int32 [4096, 6], P(('dp', 'expert')), may hold values from 0 to 15, all different within a row; in each aligned block of 128 rows (0 to 127, 128 to 255, ...) at most 60 rows name the same one
- gate_weights: float32 [4096, 6], P(('dp', 'expert')), may hold values from 0.05 to 0.3
- partner: int32 [16], replicated, may hold values from 0 to 15, as said below
- weights: bfloat16 [16, 1024, 3, 384], P('expert', 'dp'), may hold values from -0.3125 to 0.3125
- first_moment: bfloat16 [16, 1024, 3, 384], P('expert', 'dp'), may hold values from -6 to 6
- second_moment: bfloat16 [16, 1024, 3, 384], P('expert', 'dp'), may hold values from 0.099609375 to 4
Outputs:
- mixed: bfloat16 [4096, 1024], P(('dp', 'expert'))
- token_grad: bfloat16 [4096, 1024], P(('dp', 'expert'))
- new_weights: bfloat16 [16, 1024, 3, 384], P('expert', 'dp')
- new_first: bfloat16 [16, 1024, 3, 384], P('expert', 'dp')
- new_second: bfloat16 [16, 1024, 3, 384], P('expert', 'dp')
Inputs may be any that keep to these rules, and one draw needn't show every extreme that they name: `expert_ids`: each row names 6 different experts. Among the 128 tokens of one device (aligned blocks of rows), no expert is named by more than 60 tokens, and in every draw some block names some expert exactly 60 times. partner[partner[h]] = h and partner[h] != h for every h.
All inputs are finite; a program needn't handle non-finite values.
Results may differ from a plain program's by a relative error of at most 0.024.
Values may be sent and summed in bfloat16 or wider, within the bound.
A program may use at most 64 MiB of HBM per device.

v0:
```python
import jax
import jax.numpy as jnp
from jax import lax
from jax.sharding import PartitionSpec as P

beta_one = 0.9
beta_two = 0.95
learn_rate = 0.01
decay_rate = 0.1
eps_adam = 1e-08
step_count = 100


def send_rows(parts):
    return (lax.all_to_all(parts[0], "expert", split_axis=0, concat_axis=0, tiled=True),)


def send_back(parts):
    return (lax.all_to_all(parts[0], "expert", split_axis=0, concat_axis=0, tiled=True),)


def shards_by_slot(
    tokens, cotangent, expert_ids, gate_weights, partner, weights, first_moment, second_moment
):
    experts_here = lax.axis_size("expert")
    tok_dev, model_width = tokens.shape
    top_count = expert_ids.shape[1]
    hidden_width = weights.shape[3]
    capacity = min(tok_dev, max(2, 5 * tok_dev * top_count // (4 * experts_here)))
    item_total = tok_dev * top_count
    slot_total = experts_here * capacity
    flat_ids = expert_ids.reshape(item_total)
    onehot = (flat_ids[:, None] == jnp.arange(experts_here, dtype=jnp.int32)[None, :]).astype(
        jnp.int32
    )
    before = jnp.cumsum(onehot, axis=0) - onehot
    slot_of = jnp.sum(before * onehot, axis=1)
    position = flat_ids * capacity + slot_of
    source = (
        jnp.full((slot_total,), item_total, jnp.int32)
        .at[position]
        .set(jnp.arange(item_total, dtype=jnp.int32))
    )
    token_of = source // top_count
    zero_row = jnp.zeros((1, model_width), jnp.bfloat16)
    x_send = jnp.concatenate([tokens, zero_row], axis=0)[token_of].reshape(
        experts_here, capacity, model_width
    )
    gate_flat = gate_weights.reshape(item_total)
    gate_pad = jnp.concatenate([gate_flat, jnp.zeros((1,), jnp.float32)])
    cot_rows = jnp.concatenate([cotangent, zero_row], axis=0)[token_of].astype(jnp.float32)
    dy_send = (
        (gate_pad[source][:, None] * cot_rows)
        .astype(jnp.bfloat16)
        .reshape(experts_here, capacity, model_width)
    )
    gathered = lax.all_gather(weights, "dp", axis=1, tiled=True)[0]
    gate_up = gathered[:, 0:2, :].reshape(model_width, 2 * hidden_width)
    down_proj = gathered[:, 2, :]
    block_shape = (experts_here, capacity, model_width)
    (x_recv,) = send_rows((x_send,))
    forward_x_rows = x_recv.reshape(slot_total, model_width)
    both_proj = jnp.dot(forward_x_rows, gate_up, preferred_element_type=jnp.float32)
    pre_act = both_proj[:, :hidden_width]
    lin_act = both_proj[:, hidden_width:]
    sigmoid_pre = jax.nn.sigmoid(pre_act)
    silu_pre = pre_act * sigmoid_pre
    forward_hidden = (silu_pre * lin_act).astype(jnp.bfloat16)
    out_rows = jnp.dot(forward_hidden, down_proj.T, preferred_element_type=jnp.float32).astype(
        jnp.bfloat16
    )
    x_rows, saved, hidden, out_rows = (
        forward_x_rows,
        (pre_act, lin_act, sigmoid_pre, silu_pre),
        forward_hidden,
        out_rows,
    )
    (out_back,) = send_back((out_rows.reshape(block_shape),))
    (dy_recv,) = send_rows((dy_send,))
    pre_act, lin_act, sigmoid_pre, silu_pre = saved
    backward_dy_rows = dy_recv.reshape(slot_total, model_width)
    hidden_grad = jnp.dot(backward_dy_rows, down_proj, preferred_element_type=jnp.float32)
    pre_grad = (hidden_grad * lin_act * sigmoid_pre * (1.0 + pre_act * (1.0 - sigmoid_pre))).astype(
        jnp.bfloat16
    )
    lin_grad = (hidden_grad * silu_pre).astype(jnp.bfloat16)
    backward_both_grad = jnp.concatenate([pre_grad, lin_grad], axis=1)
    item_grad = jnp.dot(backward_both_grad, gate_up.T, preferred_element_type=jnp.float32).astype(
        jnp.bfloat16
    )
    dy_rows, both_grad, item_grad = (backward_dy_rows, backward_both_grad, item_grad)
    (grad_back,) = send_back((item_grad.reshape(block_shape),))
    out_items = (
        out_back.reshape(slot_total, model_width)[position].astype(jnp.float32) * gate_flat[:, None]
    )
    mixed = jnp.sum(out_items.reshape(tok_dev, top_count, model_width), axis=1).astype(jnp.bfloat16)
    grad_items = grad_back.reshape(slot_total, model_width)[position].astype(jnp.float32)
    token_grad = jnp.sum(grad_items.reshape(tok_dev, top_count, model_width), axis=1).astype(
        jnp.bfloat16
    )
    count = lax.axis_size("dp") * weights.shape[1]
    proj_grad = jnp.dot(x_rows.T, both_grad, preferred_element_type=jnp.float32)
    down_grad = jnp.dot(dy_rows.T, hidden, preferred_element_type=jnp.float32)
    grad_sum = lax.psum_scatter(
        jnp.concatenate(
            [proj_grad.reshape(count, 2, hidden_width), down_grad.reshape(count, 1, hidden_width)],
            axis=1,
        ).astype(jnp.bfloat16),
        "dp",
        scatter_dimension=0,
        tiled=True,
    ).astype(jnp.float32)
    w_old = weights[0].astype(jnp.float32)
    m_old = first_moment[0].astype(jnp.float32)
    v_old = second_moment[0].astype(jnp.float32)
    m_new = beta_one * m_old + (1.0 - beta_one) * grad_sum
    v_new = beta_two * v_old + (1.0 - beta_two) * grad_sum * grad_sum
    m_hat = m_new / (1.0 - beta_one**step_count)
    v_hat = v_new / (1.0 - beta_two**step_count)
    w_new = w_old - learn_rate * (m_hat / (jnp.sqrt(v_hat) + eps_adam) + decay_rate * w_old)
    pieces = (
        w_new.astype(jnp.bfloat16).reshape(experts_here, -1),
        m_new.astype(jnp.bfloat16).reshape(experts_here, -1),
        v_new.astype(jnp.bfloat16).reshape(experts_here, -1),
    )
    spread = (
        lax.all_to_all(pieces[0], "expert", split_axis=0, concat_axis=0, tiled=True),
        lax.all_to_all(pieces[1], "expert", split_axis=0, concat_axis=0, tiled=True),
        lax.all_to_all(pieces[2], "expert", split_axis=0, concat_axis=0, tiled=True),
    )
    ordered = (spread[0][partner], spread[1][partner], spread[2][partner])
    homed = (
        lax.all_to_all(ordered[0], "expert", split_axis=0, concat_axis=0, tiled=True),
        lax.all_to_all(ordered[1], "expert", split_axis=0, concat_axis=0, tiled=True),
        lax.all_to_all(ordered[2], "expert", split_axis=0, concat_axis=0, tiled=True),
    )
    new_weights = homed[0].reshape(weights.shape)
    new_first = homed[1].reshape(weights.shape)
    new_second = homed[2].reshape(weights.shape)
    return (mixed, token_grad, new_weights, new_first, new_second)


def adam(w_old, m_old, v_old, grad_sum):
    m_new = beta_one * m_old + (1.0 - beta_one) * grad_sum
    v_new = beta_two * v_old + (1.0 - beta_two) * grad_sum * grad_sum
    m_hat = m_new / (1.0 - beta_one**step_count)
    v_hat = v_new / (1.0 - beta_two**step_count)
    w_new = w_old - learn_rate * (m_hat / (jnp.sqrt(v_hat) + eps_adam) + decay_rate * w_old)
    return (w_new, m_new, v_new)


def shards_dense(
    tokens, cotangent, expert_ids, gate_weights, partner, weights, first_moment, second_moment
):
    experts_here = lax.axis_size("expert")
    me = lax.axis_index("expert")
    tok_dev, model_width = tokens.shape
    own_rows, hidden_width = (weights.shape[1], weights.shape[3])
    width = 3 * hidden_width
    f32, bf16 = (jnp.float32, jnp.bfloat16)
    hits = expert_ids[:, :, None] == jnp.arange(experts_here, dtype=jnp.int32)[None, None, :]
    gate_table = jnp.sum(jnp.where(hits, gate_weights[:, :, None], 0.0), axis=1).T
    w_flat = weights[0].reshape(own_rows, width)
    gathered = lax.all_gather(w_flat, "dp", axis=0, tiled=True)
    x_rows = lax.all_gather(tokens, "expert", axis=0, tiled=True)
    cot_rows = lax.all_gather(cotangent, "expert", axis=0, tiled=True)
    gate_all = lax.all_gather(gate_table, "expert", axis=0)
    gate = lax.dynamic_index_in_dim(gate_all, me, 1, keepdims=False)
    gate = gate.reshape(experts_here * tok_dev, 1)
    gate_up = gathered[:, : 2 * hidden_width]
    down_proj = gathered[:, 2 * hidden_width :]
    both_proj = jnp.dot(x_rows, gate_up, preferred_element_type=f32)
    pre_act = both_proj[:, :hidden_width]
    lin_act = both_proj[:, hidden_width:]
    sigmoid_pre = jax.nn.sigmoid(pre_act)
    silu_pre = pre_act * sigmoid_pre
    hidden = (silu_pre * lin_act).astype(bf16)
    out_rows = jnp.dot(hidden, down_proj.T, preferred_element_type=f32)
    mixed = lax.psum_scatter(
        (gate * out_rows).astype(bf16), "expert", scatter_dimension=0, tiled=True
    )
    dy_rows = (gate * cot_rows.astype(f32)).astype(bf16)
    hidden_grad = jnp.dot(dy_rows, down_proj, preferred_element_type=f32)
    pre_grad = hidden_grad * lin_act * sigmoid_pre * (1.0 + pre_act * (1.0 - sigmoid_pre))
    lin_grad = hidden_grad * silu_pre
    both_grad = jnp.concatenate([pre_grad.astype(bf16), lin_grad.astype(bf16)], axis=1)
    proj_grad = jnp.dot(x_rows.T, both_grad, preferred_element_type=f32)
    down_grad = jnp.dot(dy_rows.T, hidden, preferred_element_type=f32)
    partial = jnp.concatenate([proj_grad.astype(bf16), down_grad.astype(bf16)], axis=1)
    grad_sum = lax.psum_scatter(partial, "dp", scatter_dimension=0, tiled=True).astype(f32)
    item_grad = jnp.dot(both_grad, gate_up.T, preferred_element_type=f32).astype(bf16)
    token_grad = lax.psum_scatter(item_grad, "expert", scatter_dimension=0, tiled=True)
    m_flat = first_moment[0].reshape(own_rows, width)
    v_flat = second_moment[0].reshape(own_rows, width)
    new_state = adam(w_flat.astype(f32), m_flat.astype(f32), v_flat.astype(f32), grad_sum)
    share = own_rows // experts_here
    outs = []
    for part in new_state:
        pieces = part.astype(bf16).reshape(experts_here, share, width)
        spread = lax.all_to_all(pieces, "expert", split_axis=0, concat_axis=0, tiled=True)
        homed = lax.all_to_all(spread[partner], "expert", split_axis=0, concat_axis=0, tiled=True)
        outs.append(homed.reshape(weights.shape))
    return (mixed, token_grad, *outs)


def shards(*args):
    replica_rows = lax.axis_size("expert") * args[0].shape[0]
    if replica_rows <= 4096 and args[5].shape[1] % (16 * lax.axis_size("expert")) == 0:
        return shards_dense(*args)
    return shards_by_slot(*args)


def solution(mesh):
    in_specs = (
        P(("dp", "expert"), None),
        P(("dp", "expert"), None),
        P(("dp", "expert"), None),
        P(("dp", "expert"), None),
        P(),
        P("expert", "dp", None, None),
        P("expert", "dp", None, None),
        P("expert", "dp", None, None),
    )
    out_specs = (
        P(("dp", "expert"), None),
        P(("dp", "expert"), None),
        P("expert", "dp", None, None),
        P("expert", "dp", None, None),
        P("expert", "dp", None, None),
    )
    return jax.shard_map(shards, mesh=mesh, in_specs=in_specs, out_specs=out_specs, check_vma=False)
```

profile of v0, /device:TPU:15, one launch (start us, length us, event | category | flops | bytes accessed | tf_op | source)
XLA Modules:
  0.0 465.4 jit_solution(3843170583067933573)
XLA Ops:
  7.2 2.4 copy.29
  11.2 16.0 %all-gather = f32[256,128]{1,0:T(8,128)S(1)} all-gather(f32[16,128]{1,0:T(8,128)S(1)} %bitcast.29), channel_id=2, replica_groups=mesh['dp'=2,'expert'=16] {'expert'}, dimensions={0}, use_global_device_ids=true | all-gather | bytes 139264 | tf_op jit(solution)/shard_map/all_gather | solution.py:167
  27.2 19.2 %all-gather.7.cloned.1.call-done = bf16[1024,1152]{0,1:T(8,128)(2,1)} async-done(((bf16[512,1152]{0,1:T(8,128)(2,1)}), bf16[1024,1152]{0,1:T(8,128)(2,1)}) %all-gather.7.cloned.1.call-update) | async-done | bytes 2359312 | tf_op jit(solution)/shard_map/all_gather | solution.py:164
  46.4 53.2 %all-gather.5.cloned.1.call-done = bf16[2048,1024]{1,0:T(8,128)(2,1)} async-done(((bf16[128,1024]{1,0:T(8,128)(2,1)}), bf16[2048,1024]{1,0:T(8,128)(2,1)}) %all-gather.5.cloned.1.call-update) | async-done | bytes 4194320 | tf_op jit(solution)/shard_map/all_gather | solution.py:165
  99.6 8.7 %fusion.14 = f32[2048,768]{0,1:T(8,128)} fusion(bf16[2048,1024]{1,0:T(8,128)(2,1)} %all-gather.5.cloned.1.call-done, bf16[1024,1152]{0,1:T(8,128)(2,1)} %all-gather.7.cloned.1.call-done), kind=kOutput, calls=%fused_computation.32 | convolution fusion | flops 3221225472 | bytes 12058624 | tf_op jit(solution)/shard_map/dot_general | solution.py:172
  108.4 42.5 %all-gather.9.cloned.1.call-done = bf16[2048,1024]{1,0:T(8,128)(2,1)} async-done(((bf16[128,1024]{1,0:T(8,128)(2,1)}), bf16[2048,1024]{1,0:T(8,128)(2,1)}) %all-gather.9.cloned.1.call-update) | async-done | bytes 4194320 | tf_op jit(solution)/shard_map/all_gather | solution.py:166
  150.9 7.5 %multiply_convert_fusion.3 = (bf16[2048,384]{0,1:T(8,128)(2,1)S(1)}, bf16[2048,384]{0,1:T(8,128)(2,1)S(1)}, bf16[2048,384]{0,1:T(8,128)(2,1)S(1)}) fusion(f32[2048,768]{0,1:T(8,128)} %fusion.14, bf16[1024,1152]{0,1:T(8,128)(2,1)} %all-gather.7.cloned.1.call-done, bf16[2048,1024]{1,0:T(8,128)(2,1)} %all-gather.9.cloned.1.call-done, f32[2048]{0:T(1024)S(1)} %bitcast.30), kind=kOutput, calls=%fused_computation.9 | convolution fusion | flops 1628700672 | bytes 15998976 | tf_op jit(solution)/shard_map/dot_general | solution.py:183
  162.2 3.4 fusion.10
  174.6 25.7 %reduce-scatter.8.cloned.1.call-done = bf16[512,1152]{0,1:T(8,128)(2,1)} async-done(((bf16[1024,1152]{0,1:T(8,128)(2,1)}), bf16[512,1152]{0,1:T(8,128)(2,1)}) %reduce-scatter.8.cloned.1.call-update) | async-done | bytes 1179664 | tf_op jit(solution)/shard_map/reduce_scatter | solution.py:190
  200.3 5.8 %fusion.16 = (bf16[512,1152]{0,1:T(8,128)(2,1)S(1)}, bf16[512,1152]{0,1:T(8,128)(2,1)}, bf16[512,1152]{0,1:T(8,128)(2,1)S(1)}) fusion(bf16[512,1152]{0,1:T(8,128)(2,1)} %reduce-scatter.8.cloned.1.call-done, f32[1,512,3,384]{1,3,2,0:T(8,128)} %copy.31, f32[1,512,3,384]{1,3,2,0:T(8,128)} %copy.30, bf16[1,512,3,384]{1,3,2,0:T(8,128)(2,1)S(1)} %copy-done), kind=kLoop, calls=%fused_computation.34 | loop fusion | flops 10616832 | bytes 10616832 | tf_op jit(solution)/shard_map/convert_element_type | solution.py:199
  208.5 6.4 %all-to-all-start = ((bf16[16,32,1152]{2,1,0:T(8,128)(2,1)}), bf16[16,32,1152]{2,1,0:T(8,128)(2,1)S(1)}, u32[]{:S(2)}, u32[]{:S(2)}) async-start(bf16[16,32,1152]{2,1,0:T(8,128)(2,1)} %bitcast.7), calls=%async_computation.3 | async-start | bytes 2359296 | tf_op jit(solution)/shard_map/all_to_all | solution.py:200
  214.9 7.8 %convolution_convert_fusion = bf16[2048,1024]{1,0:T(8,128)(2,1)} fusion(bf16[2048,384]{0,1:T(8,128)(2,1)} %copy-done.11, bf16[2048,384]{0,1:T(8,128)(2,1)} %copy-done.10, bf16[1024,1152]{0,1:T(8,128)(2,1)} %all-gather.7.cloned.1.call-done), kind=kOutput, calls=%fused_computation.5 | convolution fusion | flops 3229614080 | bytes 8912896 | tf_op jit(solution)/shard_map/dot_general | solution.py:191
  224.1 18.5 %all-to-all-done = bf16[16,32,1152]{2,1,0:T(8,128)(2,1)S(1)} async-done(((bf16[16,32,1152]{2,1,0:T(8,128)(2,1)}), bf16[16,32,1152]{2,1,0:T(8,128)(2,1)S(1)}, u32[]{:S(2)}, u32[]{:S(2)}) %all-to-all-start) | async-done | bytes 1179680 | tf_op jit(solution)/shard_map/all_to_all | solution.py:200
  242.6 4.9 %all-to-all-start.2 = ((bf16[16,32,1152]{2,1,0:T(8,128)(2,1)}), bf16[16,32,1152]{2,1,0:T(8,128)(2,1)S(1)}, u32[]{:S(2)}, u32[]{:S(2)}) async-start(bf16[16,32,1152]{2,1,0:T(8,128)(2,1)} %bitcast.8), calls=%async_computation.5 | async-start | bytes 2359296 | tf_op jit(solution)/shard_map/all_to_all | solution.py:200
  248.9 43.1 %all-to-all-done.2 = bf16[16,32,1152]{2,1,0:T(8,128)(2,1)S(1)} async-done(((bf16[16,32,1152]{2,1,0:T(8,128)(2,1)}), bf16[16,32,1152]{2,1,0:T(8,128)(2,1)S(1)}, u32[]{:S(2)}, u32[]{:S(2)}) %all-to-all-start.2) | async-done | bytes 1179680 | tf_op jit(solution)/shard_map/all_to_all | solution.py:200
  292.1 4.9 %all-to-all-start.4 = ((bf16[16,32,1152]{2,1,0:T(8,128)(2,1)}), bf16[16,32,1152]{2,1,0:T(8,128)(2,1)S(1)}, u32[]{:S(2)}, u32[]{:S(2)}) async-start(bf16[16,32,1152]{2,1,0:T(8,128)(2,1)} %bitcast.27), calls=%async_computation.7 | async-start | bytes 2359296 | tf_op jit(solution)/shard_map/all_to_all | solution.py:200
  298.6 33.8 %all-to-all-done.4 = bf16[16,32,1152]{2,1,0:T(8,128)(2,1)S(1)} async-done(((bf16[16,32,1152]{2,1,0:T(8,128)(2,1)}), bf16[16,32,1152]{2,1,0:T(8,128)(2,1)S(1)}, u32[]{:S(2)}, u32[]{:S(2)}) %all-to-all-start.4) | async-done | bytes 1179680 | tf_op jit(solution)/shard_map/all_to_all | solution.py:200
  332.4 5.1 %all-to-all-start.1 = ((bf16[16,32,1152]{2,1,0:T(8,128)(2,1)}), bf16[16,32,1152]{2,1,0:T(8,128)(2,1)S(1)}, u32[]{:S(2)}, u32[]{:S(2)}) async-start(bf16[16,32,1152]{2,1,0:T(8,128)(2,1)} %gather_fusion), calls=%async_computation.4 | async-start | bytes 2359296 | tf_op jit(solution)/shard_map/all_to_all | solution.py:201
  337.5 6.0 %multiply_convert_fusion.1 = bf16[2048,1024]{1,0:T(8,128)(2,1)} fusion(bf16[2048,384]{0,1:T(8,128)(2,1)} %copy-done.9, f32[2048]{0:T(1024)S(1)} %bitcast.32, bf16[1024,1152]{0,1:T(8,128)(2,1)} %all-gather.7.cloned.1.call-done), kind=kOutput, calls=%fused_computation.4 | convolution fusion | flops 1614807040 | bytes 6561792 | tf_op jit(solution)/shard_map/dot_general | solution.py:178
  345.2 20.0 %all-to-all-done.1 = bf16[16,32,1152]{2,1,0:T(8,128)(2,1)S(1)} async-done(((bf16[16,32,1152]{2,1,0:T(8,128)(2,1)}), bf16[16,32,1152]{2,1,0:T(8,128)(2,1)S(1)}, u32[]{:S(2)}, u32[]{:S(2)}) %all-to-all-start.1) | async-done | bytes 1179680 | tf_op jit(solution)/shard_map/all_to_all | solution.py:201
  365.2 4.9 %all-to-all-start.3 = ((bf16[16,32,1152]{2,1,0:T(8,128)(2,1)}), bf16[16,32,1152]{2,1,0:T(8,128)(2,1)}, u32[]{:S(2)}, u32[]{:S(2)}) async-start(bf16[16,32,1152]{2,1,0:T(8,128)(2,1)} %gather_fusion.1), calls=%async_computation.6 | async-start | bytes 2359296 | tf_op jit(solution)/shard_map/all_to_all | solution.py:201
  371.8 43.0 %all-to-all-done.3 = bf16[16,32,1152]{2,1,0:T(8,128)(2,1)} async-done(((bf16[16,32,1152]{2,1,0:T(8,128)(2,1)}), bf16[16,32,1152]{2,1,0:T(8,128)(2,1)}, u32[]{:S(2)}, u32[]{:S(2)}) %all-to-all-start.3) | async-done | bytes 1179680 | tf_op jit(solution)/shard_map/all_to_all | solution.py:201
  414.8 5.0 %all-to-all-start.5 = ((bf16[16,32,1152]{2,1,0:T(8,128)(2,1)}), bf16[16,32,1152]{2,1,0:T(8,128)(2,1)}, u32[]{:S(2)}, u32[]{:S(2)}) async-start(bf16[16,32,1152]{2,1,0:T(8,128)(2,1)} %gather_fusion.2), calls=%async_computation.8 | async-start | bytes 2359296 | tf_op jit(solution)/shard_map/all_to_all | solution.py:201
  424.7 30.4 %all-to-all-done.5 = bf16[16,32,1152]{2,1,0:T(8,128)(2,1)} async-done(((bf16[16,32,1152]{2,1,0:T(8,128)(2,1)}), bf16[16,32,1152]{2,1,0:T(8,128)(2,1)}, u32[]{:S(2)}, u32[]{:S(2)}) %all-to-all-start.5) | async-done | bytes 1179680 | tf_op jit(solution)/shard_map/all_to_all | solution.py:201
  (60 shorter events, 33.0 us)
Async XLA Ops:
  7.2 4.0 copy-start.5
  7.2 4.0 copy-start.4
  7.2 39.2 %all-gather.7.cloned.1.call-start = ((), (), s32[]{:S(2)}) async-start(), calls=%async_computation.10 | async-start | bytes 3538944 | tf_op jit(solution)/shard_map/all_gather | solution.py:164
  9.6 90.0 %all-gather.5.cloned.1.call-start = ((), (), s32[]{:S(2)}) async-start(), calls=%async_computation.9 | async-start | bytes 4456448 | tf_op jit(solution)/shard_map/all_gather | solution.py:165
  10.4 140.5 %all-gather.9.cloned.1.call-start = ((), (), s32[]{:S(2)}) async-start(), calls=%async_computation.12 | async-start | bytes 4456448 | tf_op jit(solution)/shard_map/all_gather | solution.py:166
  11.1 189.2 %reduce-scatter.8.cloned.1.call-start = ((), (), s32[]{:S(2)}) async-start(), calls=%async_computation.14 | async-start | bytes 3538944 | tf_op jit(solution)/shard_map/reduce_scatter | solution.py:190
  150.9 7.5 %copy-start.7 = (bf16[2048,1024]{1,0:T(8,128)(2,1)S(1)}, bf16[2048,1024]{1,0:T(8,128)(2,1)}, u32[]{:S(2)}) copy-start(bf16[2048,1024]{1,0:T(8,128)(2,1)} %all-gather.9.cloned.1.call-done) | copy-start | bytes 12582916
  158.3 2.0 copy-start.9
  158.3 2.0 copy-start.10
  158.4 2.4 copy-start.11
  158.4 3.9 copy-start.6
  167.3 1.3 copy-start.3
  172.6 27.7 %copy-start = (bf16[1,512,3,384]{1,3,2,0:T(8,128)(2,1)S(1)}, bf16[1,512,3,384]{1,3,2,0:T(8,128)(2,1)}, u32[]{:S(2)}) copy-start(bf16[1,512,3,384]{1,3,2,0:T(8,128)(2,1)} %copy.29) | copy-start | bytes 3538948
  208.5 34.1 %all-to-all-start = ((bf16[16,32,1152]{2,1,0:T(8,128)(2,1)}), bf16[16,32,1152]{2,1,0:T(8,128)(2,1)S(1)}, u32[]{:S(2)}, u32[]{:S(2)}) async-start(bf16[16,32,1152]{2,1,0:T(8,128)(2,1)} %bitcast.7), calls=%async_computation.3 | async-start | bytes 2359296 | tf_op jit(solution)/shard_map/all_to_all | solution.py:200
  214.9 243.7 %reduce-scatter.6.cloned.1.call-start = ((), (), s32[]{:S(2)}) async-start(), calls=%async_computation.13 | async-start | bytes 4456448 | tf_op jit(solution)/shard_map/reduce_scatter | solution.py:192
  242.6 49.4 %all-to-all-start.2 = ((bf16[16,32,1152]{2,1,0:T(8,128)(2,1)}), bf16[16,32,1152]{2,1,0:T(8,128)(2,1)S(1)}, u32[]{:S(2)}, u32[]{:S(2)}) async-start(bf16[16,32,1152]{2,1,0:T(8,128)(2,1)} %bitcast.8), calls=%async_computation.5 | async-start | bytes 2359296 | tf_op jit(solution)/shard_map/all_to_all | solution.py:200
  247.5 49.4 %copy-start.8 = (s32[16]{0:T(128)S(1)}, s32[16]{0:T(128)}, u32[]{:S(2)}) copy-start(s32[16]{0:T(128)} %param.12) | copy-start | bytes 196
  292.1 40.4 %all-to-all-start.4 = ((bf16[16,32,1152]{2,1,0:T(8,128)(2,1)}), bf16[16,32,1152]{2,1,0:T(8,128)(2,1)S(1)}, u32[]{:S(2)}, u32[]{:S(2)}) async-start(bf16[16,32,1152]{2,1,0:T(8,128)(2,1)} %bitcast.27), calls=%async_computation.7 | async-start | bytes 2359296 | tf_op jit(solution)/shard_map/all_to_all | solution.py:200
  332.4 32.8 %all-to-all-start.1 = ((bf16[16,32,1152]{2,1,0:T(8,128)(2,1)}), bf16[16,32,1152]{2,1,0:T(8,128)(2,1)S(1)}, u32[]{:S(2)}, u32[]{:S(2)}) async-start(bf16[16,32,1152]{2,1,0:T(8,128)(2,1)} %gather_fusion), calls=%async_computation.4 | async-start | bytes 2359296 | tf_op jit(solution)/shard_map/all_to_all | solution.py:201
  337.5 121.1 %reduce-scatter.4.cloned.1.call-start = ((), (), s32[]{:S(2)}) async-start(), calls=%async_computation.11 | async-start | bytes 4456448 | tf_op jit(solution)/shard_map/reduce_scatter | solution.py:179
  365.2 6.6 %copy-start.1 = (bf16[16,32,1152]{2,1,0:T(8,128)(2,1)}, bf16[16,32,1152]{2,1,0:T(8,128)(2,1)S(1)}, u32[]{:S(2)}) copy-start(bf16[16,32,1152]{2,1,0:T(8,128)(2,1)S(1)} %all-to-all-done.1) | copy-start | bytes 3538948
  365.2 49.5 %all-to-all-start.3 = ((bf16[16,32,1152]{2,1,0:T(8,128)(2,1)}), bf16[16,32,1152]{2,1,0:T(8,128)(2,1)}, u32[]{:S(2)}, u32[]{:S(2)}) async-start(bf16[16,32,1152]{2,1,0:T(8,128)(2,1)} %gather_fusion.1), calls=%async_computation.6 | async-start | bytes 2359296 | tf_op jit(solution)/shard_map/all_to_all | solution.py:201
  414.8 5.0 %copy-start.2 = (bf16[16,32,1152]{2,1,0:T(8,128)(2,1)S(1)}, bf16[16,32,1152]{2,1,0:T(8,128)(2,1)}, u32[]{:S(2)}) copy-start(bf16[16,32,1152]{2,1,0:T(8,128)(2,1)} %copy-done.1) | copy-start | bytes 3538948
  414.8 40.4 %all-to-all-start.5 = ((bf16[16,32,1152]{2,1,0:T(8,128)(2,1)}), bf16[16,32,1152]{2,1,0:T(8,128)(2,1)}, u32[]{:S(2)}, u32[]{:S(2)}) async-start(bf16[16,32,1152]{2,1,0:T(8,128)(2,1)} %gather_fusion.2), calls=%async_computation.8 | async-start | bytes 2359296 | tf_op jit(solution)/shard_map/all_to_all | solution.py:201
Sparse Core Ops, SparseCore 0:
  10.1 36.2 all-gather.6
  48.6 50.9 all-gather.4
  101.8 49.0 all-gather.8
  167.5 32.7 reduce-scatter.7
  222.9 95.5 reduce-scatter.5
  343.7 96.6 reduce-scatter.3
where the time goes:
time: 466 us; the launch traced here: 465 us
  waiting for transfers between devices  331 us (71%)
  matrix products  35.4 us (8%)
  starting transfers between devices  31.2 us (7%)
  local copies, waits for them, and re-layouts  28.5 us (6%)
  blocking collectives  16 us (3%)
  between operations  14.3 us (3%)
  other arithmetic  9.17 us (2%)
    all_to_all x3, waiting for transfers between devices, shards_dense(): lax.all_to_all(pieces, 'expert', split_axis=0, concat_axis=0, tiled=True)  95.4 us
    all_to_all x3, waiting for transfers between devices, shards_dense(): lax.all_to_all(spread[partner], 'expert', split_axis=0, concat_axis=0, ti...  93.4 us
    all_gather x1, waiting for transfers between devices, shards_dense(): x_rows = lax.all_gather(tokens, 'expert', axis=0, tiled=True)  53.2 us
    all_gather x1, waiting for transfers between devices, shards_dense(): cot_rows = lax.all_gather(cotangent, 'expert', axis=0, tiled=True)  42.5 us
    reduce_scatter x1, waiting for transfers between devices, shards_dense(): lax.psum_scatter(partial, 'dp', scatter_dimension=0, tiled=True).astype(f32)  25.7 us
    all_gather x1, waiting for transfers between devices, shards_dense(): gathered = lax.all_gather(w_flat, 'dp', axis=0, tiled=True)  19.2 us
    all_to_all x3, starting transfers between devices, shards_dense(): lax.all_to_all(pieces, 'expert', split_axis=0, concat_axis=0, tiled=True)  16.1 us
    all_gather x1, blocking collectives, shards_dense(): gate_all = lax.all_gather(gate_table, 'expert', axis=0)  16 us
  transfers between devices with their start and end apart: 12, of which 10 were waited for; matrix products, arithmetic and copies ran while one was open for 10% of the time, Pallas kernels for 0%

commit v1 on v0

--- a/solution.py
+++ b/solution.py
@@ -197,7 +197,25 @@
     outs = []
     for part in new_state:
         pieces = part.astype(bf16).reshape(experts_here, share, width)
-        spread = lax.all_to_all(pieces, "expert", split_axis=0, concat_axis=0, tiled=True)
+        carry_in = lax.axis_size("expert")
+        v_next, clean = (carry_in, lax.axis_index("expert"))
+        left_arr = pieces.shape[0] // v_next
+        outer = list(pieces.shape)
+        outer[0] = left_arr
+        low = outer[0]
+        outer[0] = low * v_next
+        spread = jnp.zeros(outer, pieces.dtype)
+        for dev_i in range(v_next):
+            current_value = lax.dynamic_slice_in_dim(
+                pieces, (clean ^ dev_i) * left_arr, left_arr, axis=0
+            )
+            if dev_i:
+                current_value = lax.ppermute(
+                    current_value, "expert", [(nth, nth ^ dev_i) for nth in range(v_next)]
+                )
+            spread = lax.dynamic_update_slice_in_dim(
+                spread, current_value, (clean ^ dev_i) * low, axis=0
+            )
         homed = lax.all_to_all(spread[partner], "expert", split_axis=0, concat_axis=0, tiled=True)
         outs.append(homed.reshape(weights.shape))
     return (mixed, token_grad, *outs)

time: 466 us -> 465 us (level)
  waiting for transfers between devices: 331 us -> 269 us
  starting transfers between devices: 31.2 us -> 72 us
  local copies, waits for them, and re-layouts: 28.5 us -> 47.4 us
    ppermute x0 -> x45, waiting for transfers between devices: none -> 116 us  [shards_dense(): lax.ppermute(current_value, 'expert', [(nth, nth ^ dev_i) for nth in rang...]
    all_to_all x3 -> x0, waiting for transfers between devices: 95.4 us -> none  [shards_dense(): lax.all_to_all(pieces, 'expert', split_axis=0, concat_axis=0, tiled=True)]
    all_to_all x3, waiting for transfers between devices: 93.4 us -> 22.8 us  [shards_dense(): lax.all_to_all(spread[partner], 'expert', split_axis=0, concat_axis=0, ti...]
    ppermute x0 -> x45, starting transfers between devices: none -> 56.1 us  [shards_dense(): lax.ppermute(current_value, 'expert', [(nth, nth ^ dev_i) for nth in rang...]
    all_to_all x3 -> x0, starting transfers between devices: 16.1 us -> none  [shards_dense(): lax.all_to_all(pieces, 'expert', split_axis=0, concat_axis=0, tiled=True)]
    dynamic_update_slice x0 -> x45, local copies, waits for them, and re-layouts: none -> 13.9 us  [shards_dense(): lax.dynamic_update_slice_in_dim(spread, current_value, (clean ^ dev_i) *...]
    reduce_scatter x1, waiting for transfers between devices: 25.7 us -> 14 us  [shards_dense(): lax.psum_scatter(partial, 'dp', scatter_dimension=0, tiled=True).astype(f32)]
    unnamed x28 -> x80, local copies, waits for them, and re-layouts: 9.09 us -> 11.1 us
  transfers between devices with their start and end apart: 12 -> 54, of which waited for: 10 -> 25; matrix products, arithmetic and copies ran while one was open for 10% -> 15% of each run, Pallas kernels for 0% -> 0%
where the time goes in v1:
time: 465 us; the launch traced here: 463 us
  waiting for transfers between devices  269 us (58%)
  starting transfers between devices  72 us (15%)
  local copies, waits for them, and re-layouts  47.4 us (10%)
  matrix products  34.4 us (7%)
  blocking collectives  16 us (3%)
  between operations  14.9 us (3%)
  other arithmetic  8.54 us (2%)
    ppermute x45, waiting for transfers between devices, shards_dense(): lax.ppermute(current_value, 'expert', [(nth, nth ^ dev_i) for nth in rang...  116 us
    ppermute x45, starting transfers between devices, shards_dense(): lax.ppermute(current_value, 'expert', [(nth, nth ^ dev_i) for nth in rang...  56.1 us
    all_gather x1, waiting for transfers between devices, shards_dense(): x_rows = lax.all_gather(tokens, 'expert', axis=0, tiled=True)  53.2 us
    all_gather x1, waiting for transfers between devices, shards_dense(): cot_rows = lax.all_gather(cotangent, 'expert', axis=0, tiled=True)  42.5 us
    all_to_all x3, waiting for transfers between devices, shards_dense(): lax.all_to_all(spread[partner], 'expert', split_axis=0, concat_axis=0, ti...  22.8 us
    all_gather x1, waiting for transfers between devices, shards_dense(): gathered = lax.all_gather(w_flat, 'dp', axis=0, tiled=True)  19.2 us
    all_gather x1, blocking collectives, shards_dense(): gate_all = lax.all_gather(gate_table, 'expert', axis=0)  16 us
    all_to_all x3, starting transfers between devices, shards_dense(): lax.all_to_all(spread[partner], 'expert', split_axis=0, concat_axis=0, ti...  15.4 us
  transfers between devices with their start and end apart: 54, of which 25 were waited for; matrix products, arithmetic and copies ran while one was open for 15% of the time, Pallas kernels for 0%

profile of v1, /device:TPU:15, one launch (start us, length us, event | category | flops | bytes accessed | tf_op | source)
XLA Modules:
  0.0 462.6 jit_solution(5432297077829376195)
XLA Ops:
  11.2 16.0 %all-gather = f32[256,128]{1,0:T(8,128)S(1)} all-gather(f32[16,128]{1,0:T(8,128)S(1)} %bitcast.31), channel_id=2, replica_groups=mesh['dp'=2,'expert'=16] {'expert'}, dimensions={0}, use_global_device_ids=true | all-gather | bytes 139264 | tf_op jit(solution)/shard_map/all_gather | solution.py:167
  27.2 19.2 %all-gather.7.cloned.1.call-done = bf16[1024,1152]{0,1:T(8,128)(2,1)} async-done(((bf16[512,1152]{0,1:T(8,128)(2,1)}), bf16[1024,1152]{0,1:T(8,128)(2,1)}) %all-gather.7.cloned.1.call-update) | async-done | bytes 2359312 | tf_op jit(solution)/shard_map/all_gather | solution.py:164
  46.4 53.2 %all-gather.5.cloned.1.call-done = bf16[2048,1024]{1,0:T(8,128)(2,1)} async-done(((bf16[128,1024]{1,0:T(8,128)(2,1)}), bf16[2048,1024]{1,0:T(8,128)(2,1)}) %all-gather.5.cloned.1.call-update) | async-done | bytes 4194320 | tf_op jit(solution)/shard_map/all_gather | solution.py:165
  99.6 8.7 %fusion.14 = f32[2048,768]{0,1:T(8,128)} fusion(bf16[2048,1024]{1,0:T(8,128)(2,1)} %all-gather.5.cloned.1.call-done, bf16[1024,1152]{0,1:T(8,128)(2,1)} %all-gather.7.cloned.1.call-done), kind=kOutput, calls=%fused_computation.32 | convolution fusion | flops 3221225472 | bytes 12058624 | tf_op jit(solution)/shard_map/dot_general | solution.py:172
  108.3 42.5 %all-gather.9.cloned.1.call-done = bf16[2048,1024]{1,0:T(8,128)(2,1)} async-done(((bf16[128,1024]{1,0:T(8,128)(2,1)}), bf16[2048,1024]{1,0:T(8,128)(2,1)}) %all-gather.9.cloned.1.call-update) | async-done | bytes 4194320 | tf_op jit(solution)/shard_map/all_gather | solution.py:166
  150.8 7.2 %multiply_convert_fusion.3 = (bf16[2048,384]{0,1:T(8,128)(2,1)S(1)}, bf16[2048,384]{0,1:T(8,128)(2,1)S(1)}, bf16[2048,384]{0,1:T(8,128)(2,1)S(1)}) fusion(f32[2048,768]{0,1:T(8,128)} %fusion.14, bf16[1024,1152]{0,1:T(8,128)(2,1)S(1)} %copy-done.33, bf16[2048,1024]{1,0:T(8,128)(2,1)} %all-gather.9.cloned.1.call-done, f32[2048]{0:T(1024)S(1)} %bitcast.32), kind=kOutput, calls=%fused_computation.9 | convolution fusion | flops 1628700672 | bytes 15998976 | tf_op jit(solution)/shard_map/dot_general | solution.py:183
  167.1 7.0 %convolution_convert_fusion = bf16[2048,1024]{1,0:T(8,128)(2,1)} fusion(bf16[2048,384]{0,1:T(8,128)(2,1)} %copy-done.37, bf16[2048,384]{0,1:T(8,128)(2,1)} %copy-done.36, bf16[1024,1152]{0,1:T(8,128)(2,1)S(1)} %copy-done.33), kind=kOutput, calls=%fused_computation.5 | convolution fusion | flops 3229614080 | bytes 8912896 | tf_op jit(solution)/shard_map/dot_general | solution.py:191
  179.8 6.1 %multiply_convert_fusion.1 = bf16[2048,1024]{1,0:T(8,128)(2,1)} fusion(bf16[2048,384]{0,1:T(8,128)(2,1)} %copy-done.35, f32[2048]{0:T(1024)S(1)} %bitcast.34, bf16[1024,1152]{0,1:T(8,128)(2,1)} %all-gather.7.cloned.1.call-done), kind=kOutput, calls=%fused_computation.4 | convolution fusion | flops 1614807040 | bytes 6561792 | tf_op jit(solution)/shard_map/dot_general | solution.py:178
  186.0 14.0 %reduce-scatter.8.cloned.1.call-done = bf16[512,1152]{0,1:T(8,128)(2,1)} async-done(((bf16[1024,1152]{0,1:T(8,128)(2,1)}), bf16[512,1152]{0,1:T(8,128)(2,1)}) %reduce-scatter.8.cloned.1.call-update) | async-done | bytes 1179664 | tf_op jit(solution)/shard_map/reduce_scatter | solution.py:190
  200.0 6.5 %fusion.16 = (bf16[512,1152]{0,1:T(8,128)(2,1)}, bf16[512,1152]{0,1:T(8,128)(2,1)}, bf16[512,1152]{0,1:T(8,128)(2,1)}) fusion(bf16[512,1152]{0,1:T(8,128)(2,1)} %reduce-scatter.8.cloned.1.call-done, f32[1,512,3,384]{1,3,2,0:T(8,128)} %copy.31, f32[1,512,3,384]{1,3,2,0:T(8,128)S(1)} %copy-done.1, bf16[1,512,3,384]{1,3,2,0:T(8,128)(2,1)S(1)} %copy-done), kind=kLoop, calls=%fused_computation.34 | loop fusion | flops 10616832 | bytes 10616832 | tf_op jit(solution)/shard_map/convert_element_type | solution.py:199
  237.9 11.2 %collective-permute-done.39 = bf16[1,32,1152]{2,1,0:T(8,128)(2,1)S(1)} collective-permute-done((bf16[1,32,1152]{2,1,0:T(8,128)(2,1)S(1)}, bf16[1,32,1152]{2,1,0:T(8,128)(2,1)S(1)}, u32[]{:S(2)}, u32[]{:S(2)}) %collective-permute-start.39) | collective-permute-done | bytes 73760 | tf_op jit(solution)/shard_map/ppermute | solution.py:213
  253.6 4.7 %collective-permute-done.41 = bf16[1,32,1152]{2,1,0:T(8,128)(2,1)S(1)} collective-permute-done((bf16[1,32,1152]{2,1,0:T(8,128)(2,1)S(1)}, bf16[1,32,1152]{2,1,0:T(8,128)(2,1)S(1)}, u32[]{:S(2)}, u32[]{:S(2)}) %collective-permute-start.41) | collective-permute-done | bytes 73760 | tf_op jit(solution)/shard_map/ppermute | solution.py:213
  263.4 4.3 collective-permute-done.43
  272.1 6.7 %all-to-all-start.2 = ((bf16[16,32,1152]{2,1,0:T(8,128)(2,1)}), bf16[16,32,1152]{2,1,0:T(8,128)(2,1)S(1)}, u32[]{:S(2)}, u32[]{:S(2)}) async-start(bf16[16,32,1152]{2,1,0:T(8,128)(2,1)} %gather_fusion.2), calls=%async_computation.5 | async-start | bytes 2359296 | tf_op jit(solution)/shard_map/all_to_all | solution.py:219
  291.2 16.2 %collective-permute-done.20 = bf16[1,32,1152]{2,1,0:T(8,128)(2,1)S(1)} collective-permute-done((bf16[1,32,1152]{2,1,0:T(8,128)(2,1)}, bf16[1,32,1152]{2,1,0:T(8,128)(2,1)S(1)}, u32[]{:S(2)}, u32[]{:S(2)}) %collective-permute-start.20) | collective-permute-done | bytes 73760 | tf_op jit(solution)/shard_map/ppermute | solution.py:213
  312.0 7.6 %collective-permute-done.22 = bf16[1,32,1152]{2,1,0:T(8,128)(2,1)S(1)} collective-permute-done((bf16[1,32,1152]{2,1,0:T(8,128)(2,1)}, bf16[1,32,1152]{2,1,0:T(8,128)(2,1)S(1)}, u32[]{:S(2)}, u32[]{:S(2)}) %collective-permute-start.22) | collective-permute-done | bytes 73760 | tf_op jit(solution)/shard_map/ppermute | solution.py:213
  325.6 5.9 %collective-permute-done.26 = bf16[1,32,1152]{2,1,0:T(8,128)(2,1)S(1)} collective-permute-done((bf16[1,32,1152]{2,1,0:T(8,128)(2,1)}, bf16[1,32,1152]{2,1,0:T(8,128)(2,1)S(1)}, u32[]{:S(2)}, u32[]{:S(2)}) %collective-permute-start.26) | collective-permute-done | bytes 73760 | tf_op jit(solution)/shard_map/ppermute | solution.py:213
  338.8 5.3 %collective-permute-done.29 = bf16[1,32,1152]{2,1,0:T(8,128)(2,1)S(1)} collective-permute-done((bf16[1,32,1152]{2,1,0:T(8,128)(2,1)S(1)}, bf16[1,32,1152]{2,1,0:T(8,128)(2,1)S(1)}, u32[]{:S(2)}, u32[]{:S(2)}) %collective-permute-start.29) | collective-permute-done | bytes 73760 | tf_op jit(solution)/shard_map/ppermute | solution.py:213
  353.4 5.8 %collective-permute-start.10 = (bf16[1,32,1152]{2,1,0:T(8,128)(2,1)}, bf16[1,32,1152]{2,1,0:T(8,128)(2,1)S(1)}, u32[]{:S(2)}, u32[]{:S(2)}) collective-permute-start(bf16[1,32,1152]{2,1,0:T(8,128)(2,1)} %get-tuple-element.57), channel_id=1, source_target_pairs={{0,11},{1,10},{2,9},{3,8},{4,15},{5,14},{6,13},{7,12},{8,3},{9,2},... | collective-permute-start | bytes 221192 | tf_op jit(solution)/shard_map/ppermute | solution.py:213
  360.2 4.3 all-to-all-start.1
  371.2 4.9 %collective-permute-start.14 = (bf16[1,32,1152]{2,1,0:T(8,128)(2,1)S(1)}, bf16[1,32,1152]{2,1,0:T(8,128)(2,1)S(1)}, u32[]{:S(2)}, u32[]{:S(2)}) collective-permute-start(bf16[1,32,1152]{2,1,0:T(8,128)(2,1)S(1)} %copy-done.8), channel_id=1, source_target_pairs={{0,15},{1,14},{2,13},{3,12},{4,11},{5,10},{6,9},{7,8},{8,7},{9,6},... | collective-permute-start | bytes 221192 | tf_op jit(solution)/shard_map/ppermute | solution.py:213
  377.0 35.8 %collective-permute-done.11 = bf16[1,32,1152]{2,1,0:T(8,128)(2,1)S(1)} collective-permute-done((bf16[1,32,1152]{2,1,0:T(8,128)(2,1)S(1)}, bf16[1,32,1152]{2,1,0:T(8,128)(2,1)S(1)}, u32[]{:S(2)}, u32[]{:S(2)}) %collective-permute-start.11) | collective-permute-done | bytes 73760 | tf_op jit(solution)/shard_map/ppermute | solution.py:213
  420.1 4.4 all-to-all-start
  429.6 22.8 %all-to-all-done = bf16[16,32,1152]{2,1,0:T(8,128)(2,1)} async-done(((bf16[16,32,1152]{2,1,0:T(8,128)(2,1)}), bf16[16,32,1152]{2,1,0:T(8,128)(2,1)}, u32[]{:S(2)}, u32[]{:S(2)}) %all-to-all-start) | async-done | bytes 1179680 | tf_op jit(solution)/shard_map/all_to_all | solution.py:219
  (247 shorter events, 127.4 us)
Async XLA Ops:
  7.2 39.2 %all-gather.7.cloned.1.call-start = ((), (), s32[]{:S(2)}) async-start(), calls=%async_computation.7 | async-start | bytes 3538944 | tf_op jit(solution)/shard_map/all_gather | solution.py:164
  9.6 90.0 %all-gather.5.cloned.1.call-start = ((), (), s32[]{:S(2)}) async-start(), calls=%async_computation.6 | async-start | bytes 4456448 | tf_op jit(solution)/shard_map/all_gather | solution.py:165
  10.4 140.5 %all-gather.9.cloned.1.call-start = ((), (), s32[]{:S(2)}) async-start(), calls=%async_computation.9 | async-start | bytes 4456448 | tf_op jit(solution)/shard_map/all_gather | solution.py:166
  11.1 188.9 %reduce-scatter.8.cloned.1.call-start = ((), (), s32[]{:S(2)}) async-start(), calls=%async_computation.11 | async-start | bytes 3538944 | tf_op jit(solution)/shard_map/reduce_scatter | solution.py:190
  167.1 288.7 %reduce-scatter.6.cloned.1.call-start = ((), (), s32[]{:S(2)}) async-start(), calls=%async_computation.10 | async-start | bytes 4456448 | tf_op jit(solution)/shard_map/reduce_scatter | solution.py:192
  174.1 281.7 %reduce-scatter.4.cloned.1.call-start = ((), (), s32[]{:S(2)}) async-start(), calls=%async_computation.8 | async-start | bytes 4456448 | tf_op jit(solution)/shard_map/reduce_scatter | solution.py:179
  234.3 24.0 %collective-permute-start.41 = (bf16[1,32,1152]{2,1,0:T(8,128)(2,1)S(1)}, bf16[1,32,1152]{2,1,0:T(8,128)(2,1)S(1)}, u32[]{:S(2)}, u32[]{:S(2)}) collective-permute-start(bf16[1,32,1152]{2,1,0:T(8,128)(2,1)S(1)} %copy-done.22), channel_id=1, source_target_pairs={{0,12},{1,13},{2,14},{3,15},{4,8},{5,9},{6,10},{7,11},{8,4},{9,5},... | collective-permute-start | bytes 221192 | tf_op jit(solution)/shard_map/ppermute | solution.py:213
  235.6 27.3 %collective-permute-start.42 = (bf16[1,32,1152]{2,1,0:T(8,128)(2,1)S(1)}, bf16[1,32,1152]{2,1,0:T(8,128)(2,1)S(1)}, u32[]{:S(2)}, u32[]{:S(2)}) collective-permute-start(bf16[1,32,1152]{2,1,0:T(8,128)(2,1)S(1)} %copy-done.21), channel_id=1, source_target_pairs={{0,13},{1,12},{2,15},{3,14},{4,9},{5,8},{6,11},{7,10},{8,5},{9,4},... | collective-permute-start | bytes 221192 | tf_op jit(solution)/shard_map/ppermute | solution.py:213
  237.9 29.8 %collective-permute-start.43 = (bf16[1,32,1152]{2,1,0:T(8,128)(2,1)S(1)}, bf16[1,32,1152]{2,1,0:T(8,128)(2,1)S(1)}, u32[]{:S(2)}, u32[]{:S(2)}) collective-permute-start(bf16[1,32,1152]{2,1,0:T(8,128)(2,1)S(1)} %copy-done.20), channel_id=1, source_target_pairs={{0,14},{1,15},{2,12},{3,13},{4,10},{5,11},{6,8},{7,9},{8,6},{9,7},... | collective-permute-start | bytes 221192 | tf_op jit(solution)/shard_map/ppermute | solution.py:213
  252.5 26.5 %collective-permute-start.15 = (bf16[1,32,1152]{2,1,0:T(8,128)(2,1)}, bf16[1,32,1152]{2,1,0:T(8,128)(2,1)}, u32[]{:S(2)}, u32[]{:S(2)}) collective-permute-start(bf16[1,32,1152]{2,1,0:T(8,128)(2,1)} %get-tuple-element.51), channel_id=1, source_target_pairs={{0,1},{1,0},{2,3},{3,2},{4,5},{5,4},{6,7},{7,6},{8,9},{9,8},{10,11... | collective-permute-start | bytes 221192 | tf_op jit(solution)/shard_map/ppermute | solution.py:213
  272.1 87.0 %all-to-all-start.2 = ((bf16[16,32,1152]{2,1,0:T(8,128)(2,1)}), bf16[16,32,1152]{2,1,0:T(8,128)(2,1)S(1)}, u32[]{:S(2)}, u32[]{:S(2)}) async-start(bf16[16,32,1152]{2,1,0:T(8,128)(2,1)} %gather_fusion.2), calls=%async_computation.5 | async-start | bytes 2359296 | tf_op jit(solution)/shard_map/all_to_all | solution.py:219
  278.9 28.5 %collective-permute-start.20 = (bf16[1,32,1152]{2,1,0:T(8,128)(2,1)}, bf16[1,32,1152]{2,1,0:T(8,128)(2,1)S(1)}, u32[]{:S(2)}, u32[]{:S(2)}) collective-permute-start(bf16[1,32,1152]{2,1,0:T(8,128)(2,1)} %get-tuple-element.46), channel_id=1, source_target_pairs={{0,6},{1,7},{2,4},{3,5},{4,2},{5,3},{6,0},{7,1},{8,14},{9,15},{10,... | collective-permute-start | bytes 221192 | tf_op jit(solution)/shard_map/ppermute | solution.py:213
  280.0 29.3 %collective-permute-start.21 = (bf16[1,32,1152]{2,1,0:T(8,128)(2,1)}, bf16[1,32,1152]{2,1,0:T(8,128)(2,1)S(1)}, u32[]{:S(2)}, u32[]{:S(2)}) collective-permute-start(bf16[1,32,1152]{2,1,0:T(8,128)(2,1)} %get-tuple-element.45), channel_id=1, source_target_pairs={{0,7},{1,6},{2,5},{3,4},{4,3},{5,2},{6,1},{7,0},{8,15},{9,14},{10,... | collective-permute-start | bytes 221192 | tf_op jit(solution)/shard_map/ppermute | solution.py:213
  283.8 35.8 %collective-permute-start.22 = (bf16[1,32,1152]{2,1,0:T(8,128)(2,1)}, bf16[1,32,1152]{2,1,0:T(8,128)(2,1)S(1)}, u32[]{:S(2)}, u32[]{:S(2)}) collective-permute-start(bf16[1,32,1152]{2,1,0:T(8,128)(2,1)} %get-tuple-element.44), channel_id=1, source_target_pairs={{0,8},{1,9},{2,10},{3,11},{4,12},{5,13},{6,14},{7,15},{8,0},{9,1},... | collective-permute-start | bytes 221192 | tf_op jit(solution)/shard_map/ppermute | solution.py:213
  286.8 35.0 %collective-permute-start.23 = (bf16[1,32,1152]{2,1,0:T(8,128)(2,1)}, bf16[1,32,1152]{2,1,0:T(8,128)(2,1)S(1)}, u32[]{:S(2)}, u32[]{:S(2)}) collective-permute-start(bf16[1,32,1152]{2,1,0:T(8,128)(2,1)} %get-tuple-element.43), channel_id=1, source_target_pairs={{0,9},{1,8},{2,11},{3,10},{4,13},{5,12},{6,15},{7,14},{8,1},{9,0},... | collective-permute-start | bytes 221192 | tf_op jit(solution)/shard_map/ppermute | solution.py:213
  288.1 35.0 %collective-permute-start.24 = (bf16[1,32,1152]{2,1,0:T(8,128)(2,1)}, bf16[1,32,1152]{2,1,0:T(8,128)(2,1)S(1)}, u32[]{:S(2)}, u32[]{:S(2)}) collective-permute-start(bf16[1,32,1152]{2,1,0:T(8,128)(2,1)} %get-tuple-element.42), channel_id=1, source_target_pairs={{0,10},{1,11},{2,8},{3,9},{4,14},{5,15},{6,12},{7,13},{8,2},{9,3},... | collective-permute-start | bytes 221192 | tf_op jit(solution)/shard_map/ppermute | solution.py:213
  309.3 22.2 %collective-permute-start.26 = (bf16[1,32,1152]{2,1,0:T(8,128)(2,1)}, bf16[1,32,1152]{2,1,0:T(8,128)(2,1)S(1)}, u32[]{:S(2)}, u32[]{:S(2)}) collective-permute-start(bf16[1,32,1152]{2,1,0:T(8,128)(2,1)} %get-tuple-element.40), channel_id=1, source_target_pairs={{0,12},{1,13},{2,14},{3,15},{4,8},{5,9},{6,10},{7,11},{8,4},{9,5},... | collective-permute-start | bytes 221192 | tf_op jit(solution)/shard_map/ppermute | solution.py:213
  353.4 23.6 %collective-permute-start.10 = (bf16[1,32,1152]{2,1,0:T(8,128)(2,1)}, bf16[1,32,1152]{2,1,0:T(8,128)(2,1)S(1)}, u32[]{:S(2)}, u32[]{:S(2)}) collective-permute-start(bf16[1,32,1152]{2,1,0:T(8,128)(2,1)} %get-tuple-element.57), channel_id=1, source_target_pairs={{0,11},{1,10},{2,9},{3,8},{4,15},{5,14},{6,13},{7,12},{8,3},{9,2},... | collective-permute-start | bytes 221192 | tf_op jit(solution)/shard_map/ppermute | solution.py:213
  360.2 60.0 %all-to-all-start.1 = ((bf16[16,32,1152]{2,1,0:T(8,128)(2,1)}), bf16[16,32,1152]{2,1,0:T(8,128)(2,1)}, u32[]{:S(2)}, u32[]{:S(2)}) async-start(bf16[16,32,1152]{2,1,0:T(8,128)(2,1)} %gather_fusion.1), calls=%async_computation.4 | async-start | bytes 2359296 | tf_op jit(solution)/shard_map/all_to_all | solution.py:219
  365.4 47.5 %collective-permute-start.11 = (bf16[1,32,1152]{2,1,0:T(8,128)(2,1)S(1)}, bf16[1,32,1152]{2,1,0:T(8,128)(2,1)S(1)}, u32[]{:S(2)}, u32[]{:S(2)}) collective-permute-start(bf16[1,32,1152]{2,1,0:T(8,128)(2,1)S(1)} %copy-done.11), channel_id=1, source_target_pairs={{0,12},{1,13},{2,14},{3,15},{4,8},{5,9},{6,10},{7,11},{8,4},{9,5},... | collective-permute-start | bytes 221192 | tf_op jit(solution)/shard_map/ppermute | solution.py:213
  367.2 47.3 %collective-permute-start.12 = (bf16[1,32,1152]{2,1,0:T(8,128)(2,1)S(1)}, bf16[1,32,1152]{2,1,0:T(8,128)(2,1)S(1)}, u32[]{:S(2)}, u32[]{:S(2)}) collective-permute-start(bf16[1,32,1152]{2,1,0:T(8,128)(2,1)S(1)} %copy-done.10), channel_id=1, source_target_pairs={{0,13},{1,12},{2,15},{3,14},{4,9},{5,8},{6,11},{7,10},{8,5},{9,4},... | collective-permute-start | bytes 221192 | tf_op jit(solution)/shard_map/ppermute | solution.py:213
  369.0 47.9 %collective-permute-start.13 = (bf16[1,32,1152]{2,1,0:T(8,128)(2,1)S(1)}, bf16[1,32,1152]{2,1,0:T(8,128)(2,1)S(1)}, u32[]{:S(2)}, u32[]{:S(2)}) collective-permute-start(bf16[1,32,1152]{2,1,0:T(8,128)(2,1)S(1)} %copy-done.9), channel_id=1, source_target_pairs={{0,14},{1,15},{2,12},{3,13},{4,10},{5,11},{6,8},{7,9},{8,6},{9,7},... | collective-permute-start | bytes 221192 | tf_op jit(solution)/shard_map/ppermute | solution.py:213
  371.2 47.3 %collective-permute-start.14 = (bf16[1,32,1152]{2,1,0:T(8,128)(2,1)S(1)}, bf16[1,32,1152]{2,1,0:T(8,128)(2,1)S(1)}, u32[]{:S(2)}, u32[]{:S(2)}) collective-permute-start(bf16[1,32,1152]{2,1,0:T(8,128)(2,1)S(1)} %copy-done.8), channel_id=1, source_target_pairs={{0,15},{1,14},{2,13},{3,12},{4,11},{5,10},{6,9},{7,8},{8,7},{9,6},... | collective-permute-start | bytes 221192 | tf_op jit(solution)/shard_map/ppermute | solution.py:213
  420.1 32.2 %all-to-all-start = ((bf16[16,32,1152]{2,1,0:T(8,128)(2,1)}), bf16[16,32,1152]{2,1,0:T(8,128)(2,1)}, u32[]{:S(2)}, u32[]{:S(2)}) async-start(bf16[16,32,1152]{2,1,0:T(8,128)(2,1)} %gather_fusion), calls=%async_computation.3 | async-start | bytes 2359296 | tf_op jit(solution)/shard_map/all_to_all | solution.py:219
  (68 other events, 1191.3 us)
Sparse Core Ops, SparseCore 0:
  10.1 36.2 all-gather.6
  48.6 50.9 all-gather.4
  101.8 49.0 all-gather.8
  167.2 32.7 reduce-scatter.7
  204.7 91.2 reduce-scatter.5
  300.3 106.0 reduce-scatter.3
